TPU v7x, 128 devices: a whole 4x4x4 slice. The times are simulated.
128 devices in a mesh: blk: 16 (over y_lo, z, core), leaf: 8 (over y_hi, x).
Axes of the slice: x: 4, y: 4 (y_hi: 2, y_lo: 2; y = y_hi * 2 + y_lo), z: 4, core: 2. Of those that a mesh axis runs over, the one named last changes fastest.
Arguments:
- rhs: bfloat16 [64, 262144], P(None, ('blk', 'leaf')), may hold values from -6 to 6
- basis: bfloat16 [1024, 256, 128], P(('blk', 'leaf')), may hold values from -0.375 to 0.375
- near_list: int32 [1024, 6], P(('blk', 'leaf')), may hold values from 0 to 1023, as said below
- near_block: bfloat16 [1024, 6, 256, 256], P(('blk', 'leaf')), may hold values from -0.15625 to 0.15625
- local_transfer: float32 [1024, 128, 128], P(('blk', 'leaf')), may hold values from -0.1875 to 0.1875
- cross_transfer: float32 [16, 14, 128, 128], P('blk'), may hold values from -0.375 to 0.375
- coupling_list: int32 [1024, 15, 2], P(('blk', 'leaf')), may hold values from 0 to 8, as said below
- leaf_coupling: bfloat16 [1024, 15, 2, 128, 128], P(('blk', 'leaf')), may hold values from -0.09375 to 0.09375
- root_coupling: bfloat16 [16, 15, 128, 128], P('blk'), may hold values from -0.5 to 0.5
Outputs:
- product: float32 [64, 262144], P(None, ('blk', 'leaf'))
Inputs may be any that keep to these rules, and one draw needn't show every extreme that they name: near_list[g, 0] = g; every entry names a leaf of g's own subtree whose leaf node is g // 8 - 1, g // 8 or g // 8 + 1. `coupling_list`: the value 8 marks an empty slot; any other value j names the j-th leaf of the leaf node at the same position of the subtree at that offset.
All inputs are finite; a program needn't handle non-finite values.
Results may differ from a plain program's by a relative error of at most 0.0029.
Values may be sent and summed in bfloat16 or wider, within the bound.
A program may use at most 64 MiB of HBM per device.

v0:
```python
import jax
import jax.numpy as jnp
from jax import lax
from jax.sharding import PartitionSpec as P

precise = lax.Precision.HIGHEST


def from_partner(block, axis, apart):
    count = lax.axis_size(axis)
    route = []
    for low in range(count):
        high = low | 1 << apart
        if high != low and high < count:
            route += [(low, high), (high, low)]
    return lax.ppermute(block, axis, route)


def extended_2(block, sides, width):
    for axis, dim in sides:
        count = lax.axis_size(axis)
        forward = [(i, i + 1) for i in range(count - 1)]
        backward = [(target, source) for source, target in forward]
        low = lax.ppermute(
            lax.slice_in_dim(block, block.shape[dim] - width, None, axis=dim), axis, forward
        )
        high = lax.ppermute(lax.slice_in_dim(block, 0, width, axis=dim), axis, backward)
        block = jnp.concatenate([low, block, high], axis=dim)
    return block


def shifted(value, axis, steps):
    count = lax.axis_size(axis)
    pairs = [(source, (source + steps) % count) for source in range(count)]
    return lax.ppermute(value, axis, pairs)


def pick_blocks(indices, table):
    count = table.shape[0]
    onehot = (indices[:, :, None] == jnp.arange(count, dtype=jnp.int32)[None, None, :]).astype(
        table.dtype
    )
    return jnp.einsum("abj,jnx->abnx", onehot, table, preferred_element_type=jnp.float32).astype(
        table.dtype
    )


def on_device(
    rhs,
    basis,
    near_list,
    near_block,
    local_transfer,
    cross_transfer,
    coupling_list,
    leaf_coupling,
    root_coupling,
):
    nrhs_count, width = rhs.shape
    leaves, leaf_size, rank = basis.shape
    blocks = lax.axis_size("blk")
    groups = lax.axis_size("leaf")
    levels = groups.bit_length() - 1
    blk_pos = lax.axis_index("blk")
    leaf_pos = lax.axis_index("leaf")
    transfers = cross_transfer[0]
    root_mats = root_coupling[0]
    columns = rhs.reshape(nrhs_count, leaves, leaf_size)
    leaf_coef = jnp.einsum("nip,ipr->inr", columns, basis, preferred_element_type=jnp.float32)
    leaf_sent = leaf_coef.astype(jnp.bfloat16)
    node_coef = jnp.einsum(
        "inr,irq->nq",
        leaf_coef,
        local_transfer,
        precision=precise,
        preferred_element_type=jnp.float32,
    )
    heap_leaf = groups + leaf_pos
    summed = node_coef
    for level in range(levels):
        heap = jnp.right_shift(heap_leaf, level)
        matrix = lax.dynamic_index_in_dim(transfers, heap - 2, 0, keepdims=False)
        share = jnp.dot(summed, matrix, precision=precise, preferred_element_type=jnp.float32)
        summed = share + from_partner(share, "leaf", level)
    root_sent = summed.astype(jnp.bfloat16)
    rim_width = leaves * leaf_size
    extended = extended_2(rhs, (("leaf", 1),), rim_width)
    ext_blocks = extended.reshape(nrhs_count, 3 * leaves, leaf_size)
    first_leaf = (blk_pos * groups + leaf_pos) * leaves - leaves
    local_ids = near_list - first_leaf
    onehot = (
        local_ids[:, :, None] == jnp.arange(3 * leaves, dtype=jnp.int32)[None, None, :]
    ).astype(jnp.bfloat16)
    picked = jnp.einsum(
        "ikj,njp->iknp", onehot, ext_blocks, preferred_element_type=jnp.float32
    ).astype(jnp.bfloat16)
    near_out = jnp.einsum("iknp,ikpq->niq", picked, near_block, preferred_element_type=jnp.float32)

    def couple(offset_index, visit_leaf, visit_root, leaf_far, root_far):
        slot_ids = lax.dynamic_index_in_dim(coupling_list, offset_index, 1, keepdims=False)
        couplings = lax.dynamic_index_in_dim(leaf_coupling, offset_index, 1, keepdims=False)
        picked_coef = pick_blocks(slot_ids, visit_leaf)
        leaf_far = leaf_far + jnp.einsum(
            "iknr,ikrq->inq", picked_coef, couplings, preferred_element_type=jnp.float32
        )
        root_mat = lax.dynamic_index_in_dim(root_mats, offset_index, 0, keepdims=False)
        root_far = root_far + jnp.dot(visit_root, root_mat, preferred_element_type=jnp.float32)
        return (leaf_far, root_far)

    zero_leaf = jnp.zeros((leaves, nrhs_count, rank), jnp.float32)
    zero_root = jnp.zeros((nrhs_count, rank), jnp.float32)
    start = (leaf_sent, root_sent, zero_leaf, zero_root)

    def advance(offset_index, carry):
        visit_leaf, visit_root, leaf_far, root_far = carry
        visit_leaf, visit_root = shifted((visit_leaf, visit_root), "blk", 1)
        leaf_far, root_far = couple(offset_index, visit_leaf, visit_root, leaf_far, root_far)
        return (visit_leaf, visit_root, leaf_far, root_far)

    final = lax.fori_loop(0, blocks - 1, advance, start)
    leaf_far, root_far = (final[2], final[3])
    downward = root_far
    for level in range(levels - 1, -1, -1):
        heap = jnp.right_shift(heap_leaf, level)
        matrix = lax.dynamic_index_in_dim(transfers, heap - 2, 0, keepdims=False)
        downward = jnp.dot(
            downward, matrix.T, precision=precise, preferred_element_type=jnp.float32
        )
    down_leaf = jnp.einsum(
        "nq,irq->inr",
        downward,
        local_transfer,
        precision=precise,
        preferred_element_type=jnp.float32,
    )
    leaf_total = (leaf_far + down_leaf).astype(jnp.bfloat16)
    far = jnp.einsum("inr,ipr->nip", leaf_total, basis, preferred_element_type=jnp.float32)
    return (near_out + far).reshape(nrhs_count, width)


def solution(mesh):
    in_specs = (
        P(None, ("blk", "leaf")),
        P(("blk", "leaf"), None, None),
        P(("blk", "leaf"), None),
        P(("blk", "leaf"), None, None, None),
        P(("blk", "leaf"), None, None),
        P("blk", None, None, None),
        P(("blk", "leaf"), None, None),
        P(("blk", "leaf"), None, None, None, None),
        P("blk", None, None, None),
    )
    out_specs = P(None, ("blk", "leaf"))
    return jax.shard_map(
        on_device, mesh=mesh, in_specs=in_specs, out_specs=out_specs, check_vma=False
    )
```

profile of v0, /device:TPU:24, one launch (start us, length us, event | category | flops | bytes accessed | tf_op | source)
XLA Modules:
  0.0 158.0 jit_solution(15927264320961438060)
XLA Ops:
  0.0 1.4 fusion.48
  1.5 1.5 convolution_bitcast_fusion.4
  3.2 1.6 collective-permute-start.4
  4.7 2.4 %collective-permute-done.4 = f32[64,128]{1,0:T(8,128)S(1)} collective-permute-done((f32[64,128]{1,0:T(8,128)S(1)}, f32[64,128]{1,0:T(8,128)S(1)}, u32[]{:S(2)}, u32[]{:S(2)}) %collective-permute-start.4) | collective-permute-done | bytes 32800 | tf_op jit(solution)/shard_map/ppermute | solution.py:16
  7.3 3.1 %collective-permute-start.5 = (f32[64,128]{1,0:T(8,128)S(1)}, f32[64,128]{1,0:T(8,128)S(1)}, u32[]{:S(2)}, u32[]{:S(2)}) collective-permute-start(f32[64,128]{1,0:T(8,128)S(1)} %fusion.25), channel_id=1, source_target_pairs={{0,2},{2,0},{1,3},{3,1},{4,6},{6,4},{5,7},{7,5},{8,10},{10,8},{9,1... | collective-permute-start | bytes 98312 | tf_op jit(solution)/shard_map/ppermute | solution.py:16
  10.5 3.7 %collective-permute-start.3 = (bf16[64,2048]{1,0:T(8,128)(2,1)S(1)}, bf16[64,2048]{1,0:T(8,128)(2,1)S(1)}, u32[]{:S(2)}, u32[]{:S(2)}) collective-permute-start(bf16[64,2048]{1,0:T(8,128)(2,1)S(1)} %copy-done.3), channel_id=1, source_target_pairs={{1,0},{2,1},{3,2},{4,3},{5,4},{6,5},{7,6},{9,8},{10,9},{11,10},{12... | collective-permute-start | bytes 786440 | tf_op jit(solution)/shard_map/ppermute | solution.py:27
  14.2 2.1 %collective-permute-start.2 = (bf16[64,2048]{1,0:T(8,128)(2,1)S(1)}, bf16[64,2048]{1,0:T(8,128)(2,1)S(1)}, u32[]{:S(2)}, u32[]{:S(2)}) collective-permute-start(bf16[64,2048]{1,0:T(8,128)(2,1)S(1)} %copy-done.3), channel_id=1, source_target_pairs={{0,1},{1,2},{2,3},{3,4},{4,5},{5,6},{6,7},{8,9},{9,10},{10,11},{11... | collective-permute-start | bytes 786440 | tf_op jit(solution)/shard_map/ppermute | solution.py:24
  16.5 1.3 collective-permute-start.6
  18.0 8.4 %collective-permute-done.6 = f32[64,128]{1,0:T(8,128)S(1)} collective-permute-done((f32[64,128]{1,0:T(8,128)S(1)}, f32[64,128]{1,0:T(8,128)S(1)}, u32[]{:S(2)}, u32[]{:S(2)}) %collective-permute-start.6) | collective-permute-done | bytes 32800 | tf_op jit(solution)/shard_map/ppermute | solution.py:16
  26.4 124.2 %while.20 = (s32[]{:T(128)}, bf16[8,64,128]{2,1,0:T(8,128)(2,1)S(1)}, bf16[64,128]{1,0:T(8,128)(2,1)S(1)}, f32[8,64,128]{2,1,0:T(8,128)S(1)}, f32[64,128]{1,0:T(...) while((s32[]{:T(128)}, ...), condition=%wide.region_1.2_spmd.clone, body=%wide.region_0.1_spmd.clone.sunk | while | flops 37896320 | bytes 2704148 | solution.py:120
  26.5 2.0 %collective-permute-start = (bf16[8,64,128]{2,1,0:T(8,128)(2,1)S(1)}, bf16[8,64,128]{2,1,0:T(8,128)(2,1)S(1)}, u32[]{:S(2)}, u32[]{:S(2)}) collective-permute-start(bf16[8,64,128]{2,1,0:T(8,128)(2,1)S(1)} %get-tuple-element.268), channel_id=1, source_target_pairs={{0,8},{8,16},{16,24},{24,32},{32,40},{40,48},{48,56},{56,64},{64,7... | collective-permute-start | bytes 393224 | tf_op jit(solution)/shard_map/while/body/eval_jaxpr/ppermute | solution.py:35
  28.7 3.1 %collective-permute-done.1 = bf16[64,128]{1,0:T(8,128)(2,1)S(1)} collective-permute-done((bf16[64,128]{1,0:T(8,128)(2,1)S(1)}, bf16[64,128]{1,0:T(8,128)(2,1)S(1)}, u32[]{:S(2)}, u32[]{:S(2)}) %collective-permute-start.1) | collective-permute-done | bytes 16416 | tf_op jit(solution)/shard_map/while/body/eval_jaxpr/ppermute | solution.py:35
  33.4 1.3 fusion.76
  35.0 5.0 %collective-permute-done.1 = bf16[64,128]{1,0:T(8,128)(2,1)S(1)} collective-permute-done((bf16[64,128]{1,0:T(8,128)(2,1)S(1)}, bf16[64,128]{1,0:T(8,128)(2,1)S(1)}, u32[]{:S(2)}, u32[]{:S(2)}) %collective-permute-start.1) | collective-permute-done | bytes 16416 | tf_op jit(solution)/shard_map/while/body/eval_jaxpr/ppermute | solution.py:35
  40.0 0.9 fusion.77
  41.6 1.3 fusion.76
  43.3 5.0 %collective-permute-done.1 = bf16[64,128]{1,0:T(8,128)(2,1)S(1)} collective-permute-done((bf16[64,128]{1,0:T(8,128)(2,1)S(1)}, bf16[64,128]{1,0:T(8,128)(2,1)S(1)}, u32[]{:S(2)}, u32[]{:S(2)}) %collective-permute-start.1) | collective-permute-done | bytes 16416 | tf_op jit(solution)/shard_map/while/body/eval_jaxpr/ppermute | solution.py:35
  48.3 0.9 fusion.77
  49.9 1.3 fusion.76
  51.6 5.0 %collective-permute-done.1 = bf16[64,128]{1,0:T(8,128)(2,1)S(1)} collective-permute-done((bf16[64,128]{1,0:T(8,128)(2,1)S(1)}, bf16[64,128]{1,0:T(8,128)(2,1)S(1)}, u32[]{:S(2)}, u32[]{:S(2)}) %collective-permute-start.1) | collective-permute-done | bytes 16416 | tf_op jit(solution)/shard_map/while/body/eval_jaxpr/ppermute | solution.py:35
  58.2 1.3 fusion.76
  59.9 5.0 %collective-permute-done.1 = bf16[64,128]{1,0:T(8,128)(2,1)S(1)} collective-permute-done((bf16[64,128]{1,0:T(8,128)(2,1)S(1)}, bf16[64,128]{1,0:T(8,128)(2,1)S(1)}, u32[]{:S(2)}, u32[]{:S(2)}) %collective-permute-start.1) | collective-permute-done | bytes 16416 | tf_op jit(solution)/shard_map/while/body/eval_jaxpr/ppermute | solution.py:35
  66.5 1.3 fusion.76
  68.2 5.0 %collective-permute-done.1 = bf16[64,128]{1,0:T(8,128)(2,1)S(1)} collective-permute-done((bf16[64,128]{1,0:T(8,128)(2,1)S(1)}, bf16[64,128]{1,0:T(8,128)(2,1)S(1)}, u32[]{:S(2)}, u32[]{:S(2)}) %collective-permute-start.1) | collective-permute-done | bytes 16416 | tf_op jit(solution)/shard_map/while/body/eval_jaxpr/ppermute | solution.py:35
  73.2 0.9 fusion.77
  74.8 1.3 fusion.76
  76.4 5.0 %collective-permute-done.1 = bf16[64,128]{1,0:T(8,128)(2,1)S(1)} collective-permute-done((bf16[64,128]{1,0:T(8,128)(2,1)S(1)}, bf16[64,128]{1,0:T(8,128)(2,1)S(1)}, u32[]{:S(2)}, u32[]{:S(2)}) %collective-permute-start.1) | collective-permute-done | bytes 16416 | tf_op jit(solution)/shard_map/while/body/eval_jaxpr/ppermute | solution.py:35
  83.1 1.3 fusion.76
  84.7 5.0 %collective-permute-done.1 = bf16[64,128]{1,0:T(8,128)(2,1)S(1)} collective-permute-done((bf16[64,128]{1,0:T(8,128)(2,1)S(1)}, bf16[64,128]{1,0:T(8,128)(2,1)S(1)}, u32[]{:S(2)}, u32[]{:S(2)}) %collective-permute-start.1) | collective-permute-done | bytes 16416 | tf_op jit(solution)/shard_map/while/body/eval_jaxpr/ppermute | solution.py:35
  91.3 1.3 fusion.76
  93.0 5.0 %collective-permute-done.1 = bf16[64,128]{1,0:T(8,128)(2,1)S(1)} collective-permute-done((bf16[64,128]{1,0:T(8,128)(2,1)S(1)}, bf16[64,128]{1,0:T(8,128)(2,1)S(1)}, u32[]{:S(2)}, u32[]{:S(2)}) %collective-permute-start.1) | collective-permute-done | bytes 16416 | tf_op jit(solution)/shard_map/while/body/eval_jaxpr/ppermute | solution.py:35
  98.0 0.9 fusion.77
  99.6 1.3 fusion.76
  101.3 5.0 %collective-permute-done.1 = bf16[64,128]{1,0:T(8,128)(2,1)S(1)} collective-permute-done((bf16[64,128]{1,0:T(8,128)(2,1)S(1)}, bf16[64,128]{1,0:T(8,128)(2,1)S(1)}, u32[]{:S(2)}, u32[]{:S(2)}) %collective-permute-start.1) | collective-permute-done | bytes 16416 | tf_op jit(solution)/shard_map/while/body/eval_jaxpr/ppermute | solution.py:35
  106.3 0.9 fusion.77
  107.9 1.3 fusion.76
  109.6 5.0 %collective-permute-done.1 = bf16[64,128]{1,0:T(8,128)(2,1)S(1)} collective-permute-done((bf16[64,128]{1,0:T(8,128)(2,1)S(1)}, bf16[64,128]{1,0:T(8,128)(2,1)S(1)}, u32[]{:S(2)}, u32[]{:S(2)}) %collective-permute-start.1) | collective-permute-done | bytes 16416 | tf_op jit(solution)/shard_map/while/body/eval_jaxpr/ppermute | solution.py:35
  116.2 1.3 fusion.76
  117.9 5.0 %collective-permute-done.1 = bf16[64,128]{1,0:T(8,128)(2,1)S(1)} collective-permute-done((bf16[64,128]{1,0:T(8,128)(2,1)S(1)}, bf16[64,128]{1,0:T(8,128)(2,1)S(1)}, u32[]{:S(2)}, u32[]{:S(2)}) %collective-permute-start.1) | collective-permute-done | bytes 16416 | tf_op jit(solution)/shard_map/while/body/eval_jaxpr/ppermute | solution.py:35
  122.9 0.9 fusion.77
  124.5 1.3 fusion.76
  126.1 5.0 %collective-permute-done.1 = bf16[64,128]{1,0:T(8,128)(2,1)S(1)} collective-permute-done((bf16[64,128]{1,0:T(8,128)(2,1)S(1)}, bf16[64,128]{1,0:T(8,128)(2,1)S(1)}, u32[]{:S(2)}, u32[]{:S(2)}) %collective-permute-start.1) | collective-permute-done | bytes 16416 | tf_op jit(solution)/shard_map/while/body/eval_jaxpr/ppermute | solution.py:35
  132.8 1.3 fusion.76
  134.4 5.0 %collective-permute-done.1 = bf16[64,128]{1,0:T(8,128)(2,1)S(1)} collective-permute-done((bf16[64,128]{1,0:T(8,128)(2,1)S(1)}, bf16[64,128]{1,0:T(8,128)(2,1)S(1)}, u32[]{:S(2)}, u32[]{:S(2)}) %collective-permute-start.1) | collective-permute-done | bytes 16416 | tf_op jit(solution)/shard_map/while/body/eval_jaxpr/ppermute | solution.py:35
  141.0 1.3 fusion.76
  142.7 5.0 %collective-permute-done.1 = bf16[64,128]{1,0:T(8,128)(2,1)S(1)} collective-permute-done((bf16[64,128]{1,0:T(8,128)(2,1)S(1)}, bf16[64,128]{1,0:T(8,128)(2,1)S(1)}, u32[]{:S(2)}, u32[]{:S(2)}) %collective-permute-start.1) | collective-permute-done | bytes 16416 | tf_op jit(solution)/shard_map/while/body/eval_jaxpr/ppermute | solution.py:35
  149.3 1.3 fusion.76
  153.3 3.9 %fusion.14 = f32[8,8,8,256]{3,2,1,0:T(8,128)S(1)} fusion(f32[8,64,256]{2,1,0:T(8,128)S(1)} %fusion.18, bf16[8,6,256,256]{3,2,1,0:T(8,128)(2,1)} %param.14, bf16[8,6,64,256]{3,1,2,0:T(8,128)(2,1)S(1)} %fusion.39), kind=kOutput, calls=%fused_computation.20 | convolution fusion | flops 402784256 | bytes 8912896 | tf_op jit(solution)/shard_map/iknp,ikpq->niq/dot_general | solution.py:97
  (175 shorter events, 27.8 us)
Async XLA Ops:
  0.0 2.9 %copy-start = (f32[1,14,128,128]{3,2,1,0:T(8,128)S(1)}, f32[1,14,128,128]{3,2,1,0:T(8,128)}, u32[]{:S(2)}) copy-start(f32[1,14,128,128]{3,2,1,0:T(8,128)} %param.16) | copy-start | bytes 2752516
  0.0 10.4 %copy-start.3 = (bf16[64,2048]{1,0:T(8,128)(2,1)S(1)}, bf16[64,2048]{1,0:T(8,128)(2,1)}, u32[]{:S(2)}) copy-start(bf16[64,2048]{1,0:T(8,128)(2,1)} %param.11) | copy-start | bytes 786436
  0.0 17.8 %copy-start.5 = (s32[8,6]{1,0:T(8,128)S(1)}, s32[8,6]{1,0:T(8,128)}, u32[]{:S(2)}) copy-start(s32[8,6]{1,0:T(8,128)} %param.13) | copy-start | bytes 580
  0.0 17.8 %copy-start.4 = (s32[8,15,2]{1,2,0:T(2,128)S(1)}, s32[8,15,2]{1,2,0:T(2,128)}, u32[]{:S(2)}) copy-start(s32[8,15,2]{1,2,0:T(2,128)} %param.17) | copy-start | bytes 2884
  3.2 4.0 %collective-permute-start.4 = (f32[64,128]{1,0:T(8,128)S(1)}, f32[64,128]{1,0:T(8,128)S(1)}, u32[]{:S(2)}, u32[]{:S(2)}) collective-permute-start(f32[64,128]{1,0:T(8,128)S(1)} %fusion.28), channel_id=1, source_target_pairs={{0,1},{1,0},{2,3},{3,2},{4,5},{5,4},{6,7},{7,6},{8,9},{9,8},{10,11... | collective-permute-start | bytes 98312 | tf_op jit(solution)/shard_map/ppermute | solution.py:16
  7.3 9.0 %collective-permute-start.5 = (f32[64,128]{1,0:T(8,128)S(1)}, f32[64,128]{1,0:T(8,128)S(1)}, u32[]{:S(2)}, u32[]{:S(2)}) collective-permute-start(f32[64,128]{1,0:T(8,128)S(1)} %fusion.25), channel_id=1, source_target_pairs={{0,2},{2,0},{1,3},{3,1},{4,6},{6,4},{5,7},{7,5},{8,10},{10,8},{9,1... | collective-permute-start | bytes 98312 | tf_op jit(solution)/shard_map/ppermute | solution.py:16
  10.5 141.9 %collective-permute-start.3 = (bf16[64,2048]{1,0:T(8,128)(2,1)S(1)}, bf16[64,2048]{1,0:T(8,128)(2,1)S(1)}, u32[]{:S(2)}, u32[]{:S(2)}) collective-permute-start(bf16[64,2048]{1,0:T(8,128)(2,1)S(1)} %copy-done.3), channel_id=1, source_target_pairs={{1,0},{2,1},{3,2},{4,3},{5,4},{6,5},{7,6},{9,8},{10,9},{11,10},{12... | collective-permute-start | bytes 786440 | tf_op jit(solution)/shard_map/ppermute | solution.py:27
  14.2 138.2 %collective-permute-start.2 = (bf16[64,2048]{1,0:T(8,128)(2,1)S(1)}, bf16[64,2048]{1,0:T(8,128)(2,1)S(1)}, u32[]{:S(2)}, u32[]{:S(2)}) collective-permute-start(bf16[64,2048]{1,0:T(8,128)(2,1)S(1)} %copy-done.3), channel_id=1, source_target_pairs={{0,1},{1,2},{2,3},{3,4},{4,5},{5,6},{6,7},{8,9},{9,10},{10,11},{11... | collective-permute-start | bytes 786440 | tf_op jit(solution)/shard_map/ppermute | solution.py:24
  16.5 9.8 %collective-permute-start.6 = (f32[64,128]{1,0:T(8,128)S(1)}, f32[64,128]{1,0:T(8,128)S(1)}, u32[]{:S(2)}, u32[]{:S(2)}) collective-permute-start(f32[64,128]{1,0:T(8,128)S(1)} %fusion.21), channel_id=1, source_target_pairs={{0,4},{4,0},{1,5},{5,1},{2,6},{6,2},{3,7},{7,3},{8,12},{12,8},{9,1... | collective-permute-start | bytes 98312 | tf_op jit(solution)/shard_map/ppermute | solution.py:16
  26.4 125.0 %copy-start.2 = (f32[8,128,128]{2,1,0:T(8,128)S(1)}, f32[8,128,128]{2,1,0:T(8,128)}, u32[]{:S(2)}) copy-start(f32[8,128,128]{2,1,0:T(8,128)} %param.15) | copy-start | bytes 1572868
  26.4 125.7 %copy-start.1 = (bf16[8,256,128]{2,1,0:T(8,128)(2,1)S(1)}, bf16[8,256,128]{2,1,0:T(8,128)(2,1)}, u32[]{:S(2)}) copy-start(bf16[8,256,128]{2,1,0:T(8,128)(2,1)} %param.12) | copy-start | bytes 1572868
  26.4 5.3 %collective-permute-start.1 = (bf16[64,128]{1,0:T(8,128)(2,1)S(1)}, bf16[64,128]{1,0:T(8,128)(2,1)S(1)}, u32[]{:S(2)}, u32[]{:S(2)}) collective-permute-start(bf16[64,128]{1,0:T(8,128)(2,1)S(1)} %get-tuple-element.269), channel_id=1, source_target_pairs={{0,8},{8,16},{16,24},{24,32},{32,40},{40,48},{48,56},{56,64},{64,7... | collective-permute-start | bytes 49160 | tf_op jit(solution)/shard_map/while/body/eval_jaxpr/ppermute | solution.py:35
  26.5 6.7 %collective-permute-start = (bf16[8,64,128]{2,1,0:T(8,128)(2,1)S(1)}, bf16[8,64,128]{2,1,0:T(8,128)(2,1)S(1)}, u32[]{:S(2)}, u32[]{:S(2)}) collective-permute-start(bf16[8,64,128]{2,1,0:T(8,128)(2,1)S(1)} %get-tuple-element.268), channel_id=1, source_target_pairs={{0,8},{8,16},{16,24},{24,32},{32,40},{40,48},{48,56},{56,64},{64,7... | collective-permute-start | bytes 393224 | tf_op jit(solution)/shard_map/while/body/eval_jaxpr/ppermute | solution.py:35
  34.7 5.3 %collective-permute-start.1 = (bf16[64,128]{1,0:T(8,128)(2,1)S(1)}, bf16[64,128]{1,0:T(8,128)(2,1)S(1)}, u32[]{:S(2)}, u32[]{:S(2)}) collective-permute-start(bf16[64,128]{1,0:T(8,128)(2,1)S(1)} %get-tuple-element.269), channel_id=1, source_target_pairs={{0,8},{8,16},{16,24},{24,32},{32,40},{40,48},{48,56},{56,64},{64,7... | collective-permute-start | bytes 49160 | tf_op jit(solution)/shard_map/while/body/eval_jaxpr/ppermute | solution.py:35
  34.8 6.7 %collective-permute-start = (bf16[8,64,128]{2,1,0:T(8,128)(2,1)S(1)}, bf16[8,64,128]{2,1,0:T(8,128)(2,1)S(1)}, u32[]{:S(2)}, u32[]{:S(2)}) collective-permute-start(bf16[8,64,128]{2,1,0:T(8,128)(2,1)S(1)} %get-tuple-element.268), channel_id=1, source_target_pairs={{0,8},{8,16},{16,24},{24,32},{32,40},{40,48},{48,56},{56,64},{64,7... | collective-permute-start | bytes 393224 | tf_op jit(solution)/shard_map/while/body/eval_jaxpr/ppermute | solution.py:35
  43.0 5.3 %collective-permute-start.1 = (bf16[64,128]{1,0:T(8,128)(2,1)S(1)}, bf16[64,128]{1,0:T(8,128)(2,1)S(1)}, u32[]{:S(2)}, u32[]{:S(2)}) collective-permute-start(bf16[64,128]{1,0:T(8,128)(2,1)S(1)} %get-tuple-element.269), channel_id=1, source_target_pairs={{0,8},{8,16},{16,24},{24,32},{32,40},{40,48},{48,56},{56,64},{64,7... | collective-permute-start | bytes 49160 | tf_op jit(solution)/shard_map/while/body/eval_jaxpr/ppermute | solution.py:35
  43.1 6.7 %collective-permute-start = (bf16[8,64,128]{2,1,0:T(8,128)(2,1)S(1)}, bf16[8,64,128]{2,1,0:T(8,128)(2,1)S(1)}, u32[]{:S(2)}, u32[]{:S(2)}) collective-permute-start(bf16[8,64,128]{2,1,0:T(8,128)(2,1)S(1)} %get-tuple-element.268), channel_id=1, source_target_pairs={{0,8},{8,16},{16,24},{24,32},{32,40},{40,48},{48,56},{56,64},{64,7... | collective-permute-start | bytes 393224 | tf_op jit(solution)/shard_map/while/body/eval_jaxpr/ppermute | solution.py:35
  51.3 5.3 %collective-permute-start.1 = (bf16[64,128]{1,0:T(8,128)(2,1)S(1)}, bf16[64,128]{1,0:T(8,128)(2,1)S(1)}, u32[]{:S(2)}, u32[]{:S(2)}) collective-permute-start(bf16[64,128]{1,0:T(8,128)(2,1)S(1)} %get-tuple-element.269), channel_id=1, source_target_pairs={{0,8},{8,16},{16,24},{24,32},{32,40},{40,48},{48,56},{56,64},{64,7... | collective-permute-start | bytes 49160 | tf_op jit(solution)/shard_map/while/body/eval_jaxpr/ppermute | solution.py:35
  51.3 6.7 %collective-permute-start = (bf16[8,64,128]{2,1,0:T(8,128)(2,1)S(1)}, bf16[8,64,128]{2,1,0:T(8,128)(2,1)S(1)}, u32[]{:S(2)}, u32[]{:S(2)}) collective-permute-start(bf16[8,64,128]{2,1,0:T(8,128)(2,1)S(1)} %get-tuple-element.268), channel_id=1, source_target_pairs={{0,8},{8,16},{16,24},{24,32},{32,40},{40,48},{48,56},{56,64},{64,7... | collective-permute-start | bytes 393224 | tf_op jit(solution)/shard_map/while/body/eval_jaxpr/ppermute | solution.py:35
  59.5 5.3 %collective-permute-start.1 = (bf16[64,128]{1,0:T(8,128)(2,1)S(1)}, bf16[64,128]{1,0:T(8,128)(2,1)S(1)}, u32[]{:S(2)}, u32[]{:S(2)}) collective-permute-start(bf16[64,128]{1,0:T(8,128)(2,1)S(1)} %get-tuple-element.269), channel_id=1, source_target_pairs={{0,8},{8,16},{16,24},{24,32},{32,40},{40,48},{48,56},{56,64},{64,7... | collective-permute-start | bytes 49160 | tf_op jit(solution)/shard_map/while/body/eval_jaxpr/ppermute | solution.py:35
  59.6 6.7 %collective-permute-start = (bf16[8,64,128]{2,1,0:T(8,128)(2,1)S(1)}, bf16[8,64,128]{2,1,0:T(8,128)(2,1)S(1)}, u32[]{:S(2)}, u32[]{:S(2)}) collective-permute-start(bf16[8,64,128]{2,1,0:T(8,128)(2,1)S(1)} %get-tuple-element.268), channel_id=1, source_target_pairs={{0,8},{8,16},{16,24},{24,32},{32,40},{40,48},{48,56},{56,64},{64,7... | collective-permute-start | bytes 393224 | tf_op jit(solution)/shard_map/while/body/eval_jaxpr/ppermute | solution.py:35
  67.8 5.3 %collective-permute-start.1 = (bf16[64,128]{1,0:T(8,128)(2,1)S(1)}, bf16[64,128]{1,0:T(8,128)(2,1)S(1)}, u32[]{:S(2)}, u32[]{:S(2)}) collective-permute-start(bf16[64,128]{1,0:T(8,128)(2,1)S(1)} %get-tuple-element.269), channel_id=1, source_target_pairs={{0,8},{8,16},{16,24},{24,32},{32,40},{40,48},{48,56},{56,64},{64,7... | collective-permute-start | bytes 49160 | tf_op jit(solution)/shard_map/while/body/eval_jaxpr/ppermute | solution.py:35
  67.9 6.7 %collective-permute-start = (bf16[8,64,128]{2,1,0:T(8,128)(2,1)S(1)}, bf16[8,64,128]{2,1,0:T(8,128)(2,1)S(1)}, u32[]{:S(2)}, u32[]{:S(2)}) collective-permute-start(bf16[8,64,128]{2,1,0:T(8,128)(2,1)S(1)} %get-tuple-element.268), channel_id=1, source_target_pairs={{0,8},{8,16},{16,24},{24,32},{32,40},{40,48},{48,56},{56,64},{64,7... | collective-permute-start | bytes 393224 | tf_op jit(solution)/shard_map/while/body/eval_jaxpr/ppermute | solution.py:35
  76.1 5.3 %collective-permute-start.1 = (bf16[64,128]{1,0:T(8,128)(2,1)S(1)}, bf16[64,128]{1,0:T(8,128)(2,1)S(1)}, u32[]{:S(2)}, u32[]{:S(2)}) collective-permute-start(bf16[64,128]{1,0:T(8,128)(2,1)S(1)} %get-tuple-element.269), channel_id=1, source_target_pairs={{0,8},{8,16},{16,24},{24,32},{32,40},{40,48},{48,56},{56,64},{64,7... | collective-permute-start | bytes 49160 | tf_op jit(solution)/shard_map/while/body/eval_jaxpr/ppermute | solution.py:35
  76.2 6.7 %collective-permute-start = (bf16[8,64,128]{2,1,0:T(8,128)(2,1)S(1)}, bf16[8,64,128]{2,1,0:T(8,128)(2,1)S(1)}, u32[]{:S(2)}, u32[]{:S(2)}) collective-permute-start(bf16[8,64,128]{2,1,0:T(8,128)(2,1)S(1)} %get-tuple-element.268), channel_id=1, source_target_pairs={{0,8},{8,16},{16,24},{24,32},{32,40},{40,48},{48,56},{56,64},{64,7... | collective-permute-start | bytes 393224 | tf_op jit(solution)/shard_map/while/body/eval_jaxpr/ppermute | solution.py:35
  84.4 5.3 %collective-permute-start.1 = (bf16[64,128]{1,0:T(8,128)(2,1)S(1)}, bf16[64,128]{1,0:T(8,128)(2,1)S(1)}, u32[]{:S(2)}, u32[]{:S(2)}) collective-permute-start(bf16[64,128]{1,0:T(8,128)(2,1)S(1)} %get-tuple-element.269), channel_id=1, source_target_pairs={{0,8},{8,16},{16,24},{24,32},{32,40},{40,48},{48,56},{56,64},{64,7... | collective-permute-start | bytes 49160 | tf_op jit(solution)/shard_map/while/body/eval_jaxpr/ppermute | solution.py:35
  84.5 6.7 %collective-permute-start = (bf16[8,64,128]{2,1,0:T(8,128)(2,1)S(1)}, bf16[8,64,128]{2,1,0:T(8,128)(2,1)S(1)}, u32[]{:S(2)}, u32[]{:S(2)}) collective-permute-start(bf16[8,64,128]{2,1,0:T(8,128)(2,1)S(1)} %get-tuple-element.268), channel_id=1, source_target_pairs={{0,8},{8,16},{16,24},{24,32},{32,40},{40,48},{48,56},{56,64},{64,7... | collective-permute-start | bytes 393224 | tf_op jit(solution)/shard_map/while/body/eval_jaxpr/ppermute | solution.py:35
  92.7 5.3 %collective-permute-start.1 = (bf16[64,128]{1,0:T(8,128)(2,1)S(1)}, bf16[64,128]{1,0:T(8,128)(2,1)S(1)}, u32[]{:S(2)}, u32[]{:S(2)}) collective-permute-start(bf16[64,128]{1,0:T(8,128)(2,1)S(1)} %get-tuple-element.269), channel_id=1, source_target_pairs={{0,8},{8,16},{16,24},{24,32},{32,40},{40,48},{48,56},{56,64},{64,7... | collective-permute-start | bytes 49160 | tf_op jit(solution)/shard_map/while/body/eval_jaxpr/ppermute | solution.py:35
  92.7 6.7 %collective-permute-start = (bf16[8,64,128]{2,1,0:T(8,128)(2,1)S(1)}, bf16[8,64,128]{2,1,0:T(8,128)(2,1)S(1)}, u32[]{:S(2)}, u32[]{:S(2)}) collective-permute-start(bf16[8,64,128]{2,1,0:T(8,128)(2,1)S(1)} %get-tuple-element.268), channel_id=1, source_target_pairs={{0,8},{8,16},{16,24},{24,32},{32,40},{40,48},{48,56},{56,64},{64,7... | collective-permute-start | bytes 393224 | tf_op jit(solution)/shard_map/while/body/eval_jaxpr/ppermute | solution.py:35
  100.9 5.3 %collective-permute-start.1 = (bf16[64,128]{1,0:T(8,128)(2,1)S(1)}, bf16[64,128]{1,0:T(8,128)(2,1)S(1)}, u32[]{:S(2)}, u32[]{:S(2)}) collective-permute-start(bf16[64,128]{1,0:T(8,128)(2,1)S(1)} %get-tuple-element.269), channel_id=1, source_target_pairs={{0,8},{8,16},{16,24},{24,32},{32,40},{40,48},{48,56},{56,64},{64,7... | collective-permute-start | bytes 49160 | tf_op jit(solution)/shard_map/while/body/eval_jaxpr/ppermute | solution.py:35
  101.0 6.7 %collective-permute-start = (bf16[8,64,128]{2,1,0:T(8,128)(2,1)S(1)}, bf16[8,64,128]{2,1,0:T(8,128)(2,1)S(1)}, u32[]{:S(2)}, u32[]{:S(2)}) collective-permute-start(bf16[8,64,128]{2,1,0:T(8,128)(2,1)S(1)} %get-tuple-element.268), channel_id=1, source_target_pairs={{0,8},{8,16},{16,24},{24,32},{32,40},{40,48},{48,56},{56,64},{64,7... | collective-permute-start | bytes 393224 | tf_op jit(solution)/shard_map/while/body/eval_jaxpr/ppermute | solution.py:35
  109.2 5.3 %collective-permute-start.1 = (bf16[64,128]{1,0:T(8,128)(2,1)S(1)}, bf16[64,128]{1,0:T(8,128)(2,1)S(1)}, u32[]{:S(2)}, u32[]{:S(2)}) collective-permute-start(bf16[64,128]{1,0:T(8,128)(2,1)S(1)} %get-tuple-element.269), channel_id=1, source_target_pairs={{0,8},{8,16},{16,24},{24,32},{32,40},{40,48},{48,56},{56,64},{64,7... | collective-permute-start | bytes 49160 | tf_op jit(solution)/shard_map/while/body/eval_jaxpr/ppermute | solution.py:35
  109.3 6.7 %collective-permute-start = (bf16[8,64,128]{2,1,0:T(8,128)(2,1)S(1)}, bf16[8,64,128]{2,1,0:T(8,128)(2,1)S(1)}, u32[]{:S(2)}, u32[]{:S(2)}) collective-permute-start(bf16[8,64,128]{2,1,0:T(8,128)(2,1)S(1)} %get-tuple-element.268), channel_id=1, source_target_pairs={{0,8},{8,16},{16,24},{24,32},{32,40},{40,48},{48,56},{56,64},{64,7... | collective-permute-start | bytes 393224 | tf_op jit(solution)/shard_map/while/body/eval_jaxpr/ppermute | solution.py:35
  117.5 5.3 %collective-permute-start.1 = (bf16[64,128]{1,0:T(8,128)(2,1)S(1)}, bf16[64,128]{1,0:T(8,128)(2,1)S(1)}, u32[]{:S(2)}, u32[]{:S(2)}) collective-permute-start(bf16[64,128]{1,0:T(8,128)(2,1)S(1)} %get-tuple-element.269), channel_id=1, source_target_pairs={{0,8},{8,16},{16,24},{24,32},{32,40},{40,48},{48,56},{56,64},{64,7... | collective-permute-start | bytes 49160 | tf_op jit(solution)/shard_map/while/body/eval_jaxpr/ppermute | solution.py:35
  117.6 6.7 %collective-permute-start = (bf16[8,64,128]{2,1,0:T(8,128)(2,1)S(1)}, bf16[8,64,128]{2,1,0:T(8,128)(2,1)S(1)}, u32[]{:S(2)}, u32[]{:S(2)}) collective-permute-start(bf16[8,64,128]{2,1,0:T(8,128)(2,1)S(1)} %get-tuple-element.268), channel_id=1, source_target_pairs={{0,8},{8,16},{16,24},{24,32},{32,40},{40,48},{48,56},{56,64},{64,7... | collective-permute-start | bytes 393224 | tf_op jit(solution)/shard_map/while/body/eval_jaxpr/ppermute | solution.py:35
  125.8 5.3 %collective-permute-start.1 = (bf16[64,128]{1,0:T(8,128)(2,1)S(1)}, bf16[64,128]{1,0:T(8,128)(2,1)S(1)}, u32[]{:S(2)}, u32[]{:S(2)}) collective-permute-start(bf16[64,128]{1,0:T(8,128)(2,1)S(1)} %get-tuple-element.269), channel_id=1, source_target_pairs={{0,8},{8,16},{16,24},{24,32},{32,40},{40,48},{48,56},{56,64},{64,7... | collective-permute-start | bytes 49160 | tf_op jit(solution)/shard_map/while/body/eval_jaxpr/ppermute | solution.py:35
  125.9 6.7 %collective-permute-start = (bf16[8,64,128]{2,1,0:T(8,128)(2,1)S(1)}, bf16[8,64,128]{2,1,0:T(8,128)(2,1)S(1)}, u32[]{:S(2)}, u32[]{:S(2)}) collective-permute-start(bf16[8,64,128]{2,1,0:T(8,128)(2,1)S(1)} %get-tuple-element.268), channel_id=1, source_target_pairs={{0,8},{8,16},{16,24},{24,32},{32,40},{40,48},{48,56},{56,64},{64,7... | collective-permute-start | bytes 393224 | tf_op jit(solution)/shard_map/while/body/eval_jaxpr/ppermute | solution.py:35
  134.1 5.3 %collective-permute-start.1 = (bf16[64,128]{1,0:T(8,128)(2,1)S(1)}, bf16[64,128]{1,0:T(8,128)(2,1)S(1)}, u32[]{:S(2)}, u32[]{:S(2)}) collective-permute-start(bf16[64,128]{1,0:T(8,128)(2,1)S(1)} %get-tuple-element.269), channel_id=1, source_target_pairs={{0,8},{8,16},{16,24},{24,32},{32,40},{40,48},{48,56},{56,64},{64,7... | collective-permute-start | bytes 49160 | tf_op jit(solution)/shard_map/while/body/eval_jaxpr/ppermute | solution.py:35
  134.2 6.7 %collective-permute-start = (bf16[8,64,128]{2,1,0:T(8,128)(2,1)S(1)}, bf16[8,64,128]{2,1,0:T(8,128)(2,1)S(1)}, u32[]{:S(2)}, u32[]{:S(2)}) collective-permute-start(bf16[8,64,128]{2,1,0:T(8,128)(2,1)S(1)} %get-tuple-element.268), channel_id=1, source_target_pairs={{0,8},{8,16},{16,24},{24,32},{32,40},{40,48},{48,56},{56,64},{64,7... | collective-permute-start | bytes 393224 | tf_op jit(solution)/shard_map/while/body/eval_jaxpr/ppermute | solution.py:35
  142.4 5.3 %collective-permute-start.1 = (bf16[64,128]{1,0:T(8,128)(2,1)S(1)}, bf16[64,128]{1,0:T(8,128)(2,1)S(1)}, u32[]{:S(2)}, u32[]{:S(2)}) collective-permute-start(bf16[64,128]{1,0:T(8,128)(2,1)S(1)} %get-tuple-element.269), channel_id=1, source_target_pairs={{0,8},{8,16},{16,24},{24,32},{32,40},{40,48},{48,56},{56,64},{64,7... | collective-permute-start | bytes 49160 | tf_op jit(solution)/shard_map/while/body/eval_jaxpr/ppermute | solution.py:35
  142.4 6.7 %collective-permute-start = (bf16[8,64,128]{2,1,0:T(8,128)(2,1)S(1)}, bf16[8,64,128]{2,1,0:T(8,128)(2,1)S(1)}, u32[]{:S(2)}, u32[]{:S(2)}) collective-permute-start(bf16[8,64,128]{2,1,0:T(8,128)(2,1)S(1)} %get-tuple-element.268), channel_id=1, source_target_pairs={{0,8},{8,16},{16,24},{24,32},{32,40},{40,48},{48,56},{56,64},{64,7... | collective-permute-start | bytes 393224 | tf_op jit(solution)/shard_map/while/body/eval_jaxpr/ppermute | solution.py:35
where the time goes:
time: 160 us; the launch traced here: 158 us
  waiting for transfers between devices  91.6 us (57%)
  matrix products  45.3 us (28%)
  starting transfers between devices  16 us (10%)
  local copies, waits for them, and re-layouts  2.68 us (2%)
    ppermute x30, waiting for transfers between devices, shifted(): return lax.ppermute(value, axis, pairs)  80.8 us
    dot_general x15, matrix products, couple(): jnp.einsum('iknr,ikrq->inq', picked_coef, couplings, preferred_element_ty...  19.2 us
    dot_general x15, matrix products, couple(): jnp.dot(visit_root, root_mat, preferred_element_type=jnp.float32)  13.3 us
    ppermute x3, waiting for transfers between devices, from_partner(): return lax.ppermute(block, axis, route)  10.8 us
    ppermute x3, starting transfers between devices, from_partner(): return lax.ppermute(block, axis, route)  6 us
    ppermute x30, starting transfers between devices, shifted(): return lax.ppermute(value, axis, pairs)  4.18 us
    dot_general x1, matrix products, on_device(): jnp.einsum('iknp,ikpq->niq', picked, near_block, preferred_element_type=j...  3.9 us
    ppermute x1, starting transfers between devices, extended_2(): lax.ppermute(lax.slice_in_dim(block, 0, width, axis=dim), axis, backward)  3.71 us
  transfers between devices with their start and end apart: 35, of which 32 were waited for; matrix products, arithmetic and copies ran while one was open for 26% of the time, Pallas kernels for 0%

commit v1 on v0

v1 whole, which is shorter than its diff:
```python
import jax
import jax.numpy as jnp
from jax import lax
from jax.experimental import pallas as pl
from jax.experimental.pallas import tpu as pltpu
from jax.sharding import PartitionSpec as P

bf16, f32 = jnp.bfloat16, jnp.float32

N_BLK, N_LEAF = 16, 8
LEAVES, SIZE, RANK, NRHS = 8, 256, 128, 64
NEAR, SLOTS, STEPS = 6, 2, 15
ROWS = NRHS // N_LEAF

SOURCES = [
    (dy, dz, dc) for dz in (0, -1, 1, 2) for dy in (0, 1) for dc in (0, 1) if (dy, dz, dc) != (0, 0, 0)
]


def mm(a, b):
    return jnp.dot(a, b, preferred_element_type=f32)


def mm_t(a, b):
    return lax.dot_general(a, b, (((1,), (1,)), ((), ())), preferred_element_type=f32)


def split(v):
    high = v.astype(bf16)
    return high, (v - high.astype(f32)).astype(bf16)


def mm3(a_high, a_low, b_high, b_low, product=mm):
    rows = a_high.shape[0]
    both = product(jnp.concatenate([a_high, a_low], axis=0), b_high)
    return both[:rows] + both[rows:] + product(a_high, b_low)


def kernel(
    rhs, basis_hbm, near_list, near_hbm, lt_hbm, ct_hbm, coupling_list, coup_hbm, rc_hbm,
    out,
    x, basis, nlist, near_w, lt, ct, clist, coup, rc,
    own, share_buf, rs_buf, root_own, vis, rf, far_acc, prod,
    lt_h, lt_l, t_h, t_l, g_h, g_l,
    *rest,
):
    bufs = dict(zip(SOURCES, rest[: len(SOURCES)]))
    lsem, osem, barrier_unused, hs, hr, cs, cr, rs_s, rs_r, ag_s, ag_r, al_s, al_r = rest[len(SOURCES):]
    b = lax.axis_index("blk")
    l = lax.axis_index("leaf")
    core = b % 2
    z = (b // 2) % 4
    y = b // 8

    def blk_of(dy, dz, dc):
        yy = (y + dy) % 2
        zz = (z + dz + 4) % 4
        cc = (core + dc) % 2
        return yy * 8 + zz * 2 + cc

    barrier = pltpu.get_barrier_semaphore()
    for s in range(1, N_BLK):
        pl.semaphore_signal(barrier, inc=1, device_id={"blk": (b + s) % N_BLK})
    for d in range(1, N_LEAF):
        pl.semaphore_signal(barrier, inc=1, device_id={"leaf": (l + d) % N_LEAF})

    def load(src, dst, i):
        c = pltpu.make_async_copy(src, dst, lsem.at[i])
        c.start()
        return c

    x_loads = [
        load(rhs.at[:, pl.ds(g * SIZE, SIZE)], x.at[LEAVES + g], g) for g in range(LEAVES)
    ]
    basis_load = load(basis_hbm, basis, 8)
    ct_loads = [
        load(ct_hbm.at[0, 6 + l], ct.at[0], 9),
        load(ct_hbm.at[0, 2 + l // 2], ct.at[1], 10),
        load(ct_hbm.at[0, l // 4], ct.at[2], 11),
    ]
    lt_load = load(lt_hbm, lt, 12)
    nlist_load = load(near_list, nlist, 13)
    clist_load = load(coupling_list, clist, 14)
    near_loads = [load(near_hbm.at[g], near_w.at[g], 15 + g) for g in range(LEAVES)]
    rc_load = load(rc_hbm, rc, 23)
    coup_loads = [load(coup_hbm.at[g], coup.at[g], 24 + g) for g in range(LEAVES)]

    for src in SOURCES:
        bufs[src][LEAVES] = jnp.zeros((NRHS, RANK), bf16)

    for c in x_loads:
        c.wait()
    basis_load.wait()
    coef = []
    for g in range(LEAVES):
        c = mm(x[LEAVES + g], basis[g])
        coef.append(c)
        own[g] = c.astype(bf16)

    def blk_copy(src, dst, i, dy, dz, dc):
        return pltpu.make_async_remote_copy(
            src_ref=src, dst_ref=dst, send_sem=cs.at[i], recv_sem=cr.at[i],
            device_id={"blk": blk_of(dy, dz, dc)},
        )

    whole = pl.ds(0, LEAVES)
    first, second = pl.ds(0, LEAVES // 2), pl.ds(LEAVES // 2, LEAVES // 2)
    copies = {}

    def send(name, src, target, part, dy, dz, dc):
        i = len(copies)
        c = blk_copy(src.at[part], bufs[target].at[part], i, dy, dz, dc)
        copies[name] = c
        c.start()

    pl.semaphore_wait(barrier, N_BLK - 1 + N_LEAF - 1)
    send("zp", own, (0, -1, 0), whole, 0, 1, 0)
    send("zm", own, (0, 1, 0), whole, 0, -1, 0)
    send("p", own, (0, 0, 1), whole, 0, 0, 1)

    for c in ct_loads:
        c.wait()
    lt_load.wait()
    w_h, w_l = split(lt[...].reshape(LEAVES * RANK, RANK))
    lt_h[...] = w_h
    lt_l[...] = w_l
    m0, m1, m2 = [split(ct[i]) for i in range(3)]
    t = split(mm3(*m0, *m1))
    t = split(mm3(*t, *m2))
    t_h[...], t_l[...] = t
    parts = [split(c) for c in coef]
    c_h = jnp.concatenate([p[0] for p in parts], axis=1)
    c_l = jnp.concatenate([p[1] for p in parts], axis=1)
    node = mm3(c_h, c_l, lt_h[...], lt_l[...])
    share = mm3(*split(node), *t)
    share_buf[...] = share.reshape(N_LEAF, ROWS, RANK)

    rs = []
    for d in range(1, N_LEAF):
        to = (l + d) % N_LEAF
        c = pltpu.make_async_remote_copy(
            src_ref=share_buf.at[to], dst_ref=rs_buf.at[d - 1],
            send_sem=rs_s.at[d - 1], recv_sem=rs_r.at[d - 1], device_id={"leaf": to},
        )
        c.start()
        rs.append(c)
    send("y", own, (1, 0, 0), whole, 1, 0, 0)

    mine, low, high = pl.ds(LEAVES, LEAVES), pl.ds(0, LEAVES), pl.ds(2 * LEAVES, LEAVES)
    up = pltpu.make_async_remote_copy(
        src_ref=x.at[mine], dst_ref=x.at[low], send_sem=hs.at[0], recv_sem=hr.at[0],
        device_id={"leaf": (l + 1) % N_LEAF},
    )
    down = pltpu.make_async_remote_copy(
        src_ref=x.at[mine], dst_ref=x.at[high], send_sem=hs.at[1], recv_sem=hr.at[1],
        device_id={"leaf": (l + N_LEAF - 1) % N_LEAF},
    )
    has_up, has_down = l < N_LEAF - 1, l > 0
    pl.when(has_up)(up.start)
    pl.when(has_down)(down.start)

    for c in near_loads:
        c.wait()

    def near_own(g, _):
        prod[g] = mm(x[LEAVES + g], near_w[g, pl.ds(0, SIZE), :])
        return 0

    lax.fori_loop(0, LEAVES, near_own, 0, unroll=True)

    copies["zp"].wait_recv()
    send("zp_fwd", bufs[0, -1, 0], (0, 2, 0), first, 0, 1, 0)
    send("zp_p", bufs[0, -1, 0], (0, -1, 1), whole, 0, 0, 1)
    copies["zm"].wait_recv()
    send("zm_fwd", bufs[0, 1, 0], (0, 2, 0), second, 0, -1, 0)
    send("zm_p", bufs[0, 1, 0], (0, 1, 1), whole, 0, 0, 1)
    copies["y"].wait_recv()
    send("yzp", bufs[1, 0, 0], (1, -1, 0), whole, 0, 1, 0)
    send("yzm", bufs[1, 0, 0], (1, 1, 0), whole, 0, -1, 0)
    send("y_p", bufs[1, 0, 0], (1, 0, 1), whole, 0, 0, 1)

    total = share_buf[l]
    for d in range(1, N_LEAF):
        rs[d - 1].wait_recv()
        total = total + rs_buf[d - 1]
    root_own[...] = total.astype(bf16).astype(f32)
    ag = []
    for s in range(1, N_BLK):
        c = pltpu.make_async_remote_copy(
            src_ref=root_own, dst_ref=vis.at[s - 1],
            send_sem=ag_s.at[s - 1], recv_sem=ag_r.at[s - 1], device_id={"blk": (b + s) % N_BLK},
        )
        c.start()
        ag.append(c)

    clist_load.wait()
    for c in coup_loads:
        c.wait()

    def couple(sources, fresh):
        offsets = [(b - blk_of(*src) + N_BLK) % N_BLK - 1 for src in sources]

        def body(g, _):
            total = None if fresh else far_acc[g]
            for src, o in zip(sources, offsets):
                buf = bufs[src]
                lhs = jnp.concatenate([buf[clist[g, 0, o]], buf[clist[g, 1, o]]], axis=1)
                term = mm(lhs, coup[g, o])
                total = term if total is None else total + term
            far_acc[g] = total
            return 0

        lax.fori_loop(0, LEAVES, body, 0)

    copies["p"].wait_recv()
    couple([(0, 0, 1), (1, 0, 0), (0, -1, 0), (0, 1, 0)], True)

    copies["yzp"].wait_recv()
    send("yzp_fwd", bufs[1, -1, 0], (1, 2, 0), first, 0, 1, 0)
    send("yzp_p", bufs[1, -1, 0], (1, -1, 1), whole, 0, 0, 1)
    copies["yzm"].wait_recv()
    send("yzm_fwd", bufs[1, 1, 0], (1, 2, 0), second, 0, -1, 0)
    send("yzm_p", bufs[1, 1, 0], (1, 1, 1), whole, 0, 0, 1)
    copies["zp_fwd"].wait_recv()
    copies["zm_fwd"].wait_recv()
    send("z2_p", bufs[0, 2, 0], (0, 2, 1), whole, 0, 0, 1)

    rc_load.wait()
    for c in ag:
        c.wait_recv()
    lhs = jnp.concatenate([vis[s].astype(bf16) for s in range(STEPS)], axis=1)
    rows = mm(lhs, rc[...])
    rf[l] = rows
    al = []
    for d in range(1, N_LEAF):
        c = pltpu.make_async_remote_copy(
            src_ref=rf.at[l], dst_ref=rf.at[l],
            send_sem=al_s.at[d - 1], recv_sem=al_r.at[d - 1], device_id={"leaf": (l + d) % N_LEAF},
        )
        c.start()
        al.append(c)

    nlist_load.wait()
    pl.when(has_down)(up.wait_recv)
    pl.when(has_up)(down.wait_recv)
    base = (b * N_LEAF + l) * LEAVES - LEAVES

    def near_rest(g, _):
        lhs = jnp.concatenate([x[jnp.clip(nlist[g, k] - base, 0, 3 * LEAVES - 1)] for k in range(1, NEAR)], axis=1)
        prod[g] = prod[g] + mm(lhs, near_w[g, pl.ds(SIZE, (NEAR - 1) * SIZE), :])
        return 0

    lax.fori_loop(0, LEAVES, near_rest, 0)

    for name in ("y_p", "zp_p", "zm_p"):
        copies[name].wait_recv()
    couple([(1, 0, 1), (0, -1, 1), (0, 1, 1), (1, -1, 0), (1, 1, 0), (0, 2, 0)], False)

    copies["yzp_fwd"].wait_recv()
    copies["yzm_fwd"].wait_recv()
    send("yz2_p", bufs[1, 2, 0], (1, 2, 1), whole, 0, 0, 1)

    g = split(mm3(lt_h[...], lt_l[...], t_h[...], t_l[...]))
    g_h[...], g_l[...] = g

    for name in ("yzp_p", "yzm_p", "z2_p"):
        copies[name].wait_recv()
    couple([(1, -1, 1), (1, 1, 1), (0, 2, 1), (1, 2, 0)], False)
    copies["yz2_p"].wait_recv()
    couple([(1, 2, 1)], False)

    for c in al:
        c.wait_recv()
    r_h, r_l = split(rf[...].reshape(NRHS, RANK))
    down_leaf = mm3(r_h, r_l, g_h[...], g_l[...], mm_t)
    stores = []
    for g in range(LEAVES):
        leaf_total = (far_acc[g] + down_leaf[:, g * RANK:(g + 1) * RANK]).astype(bf16)
        prod[g] = prod[g] + mm_t(leaf_total, basis[g])
        c = pltpu.make_async_copy(prod.at[g], out.at[:, pl.ds(g * SIZE, SIZE)], osem.at[g])
        c.start()
        stores.append(c)

    for c in list(copies.values()) + rs + ag + al:
        c.wait_send()
    pl.when(has_up)(up.wait_send)
    pl.when(has_down)(down.wait_send)
    for c in stores:
        c.wait()


def on_device(rhs, basis, near_list, near_block, local_transfer, cross_transfer, coupling_list, leaf_coupling, root_coupling):
    near_w = near_block.reshape(LEAVES, NEAR * SIZE, SIZE)
    coup = leaf_coupling.reshape(LEAVES, STEPS, SLOTS * RANK, RANK)
    rc = root_coupling.reshape(STEPS * RANK, RANK)
    V, S = pltpu.VMEM, pltpu.SemaphoreType
    dma = S.DMA
    scratch = [
        V((3 * LEAVES, NRHS, SIZE), bf16),
        V((LEAVES, SIZE, RANK), bf16),
        pltpu.SMEM((LEAVES, NEAR), jnp.int32),
        V((LEAVES, NEAR * SIZE, SIZE), bf16),
        V((LEAVES, RANK, RANK), f32),
        V((3, RANK, RANK), f32),
        pltpu.SMEM((LEAVES, SLOTS, STEPS), jnp.int32),
        V((LEAVES, STEPS, SLOTS * RANK, RANK), bf16),
        V((STEPS * RANK, RANK), bf16),
        V((LEAVES, NRHS, RANK), bf16),
        V((N_LEAF, ROWS, RANK), f32),
        V((N_LEAF - 1, ROWS, RANK), f32),
        V((ROWS, RANK), f32),
        V((STEPS, ROWS, RANK), f32),
        V((N_LEAF, ROWS, RANK), f32),
        V((LEAVES, NRHS, RANK), f32),
        V((LEAVES, NRHS, SIZE), f32),
        V((LEAVES * RANK, RANK), bf16),
        V((LEAVES * RANK, RANK), bf16),
        V((RANK, RANK), bf16),
        V((RANK, RANK), bf16),
        V((LEAVES * RANK, RANK), bf16),
        V((LEAVES * RANK, RANK), bf16),
    ]
    scratch += [V((LEAVES + 1, NRHS, RANK), bf16) for _ in SOURCES]
    scratch += [
        dma((32,)), dma((LEAVES,)), S.REGULAR, dma((2,)), dma((2,)), dma((17,)), dma((17,)),
        dma((7,)), dma((7,)), dma((15,)), dma((15,)), dma((7,)), dma((7,)),
    ]
    hbm = pl.BlockSpec(memory_space=pltpu.MemorySpace.HBM)
    return pl.pallas_call(
        kernel,
        out_shape=jax.ShapeDtypeStruct((NRHS, LEAVES * SIZE), f32),
        in_specs=[hbm] * 9,
        out_specs=pl.BlockSpec(memory_space=pltpu.VMEM),
        scratch_shapes=scratch,
        compiler_params=pltpu.CompilerParams(
            collective_id=0, has_side_effects=True, vmem_limit_bytes=67043328
        ),
    )(rhs, basis, near_list, near_w, local_transfer, cross_transfer, coupling_list.transpose(0, 2, 1), coup, rc)


def solution(mesh):
    both = ("blk", "leaf")
    in_specs = (
        P(None, both), P(both, None, None), P(both, None), P(both, None, None, None), P(both, None, None),
        P("blk", None, None, None), P(both, None, None), P(both, None, None, None, None), P("blk", None, None, None),
    )
    return jax.shard_map(on_device, mesh=mesh, in_specs=in_specs, out_specs=P(None, both), check_vma=False)
```

time: 160 us -> 38.2 us (0.24)
  the two profiles are of different devices: /device:TPU:24 before, /device:TPU:1 now
where the time goes in v1:
time: 38.2 us; the launch traced here: 38.1 us
  Pallas kernels  36.2 us (95%)
  local copies, waits for them, and re-layouts  1.87 us (5%)
    pallas_call x1, Pallas kernels, on_device(): pl.pallas_call(kernel, out_shape=jax.ShapeDtypeStruct((NRHS, LEAVES * SIZ...  36.2 us
    unnamed x1, local copies, waits for them, and re-layouts  1.87 us

profile of v1, /device:TPU:1, one launch (start us, length us, event | category | flops | bytes accessed | tf_op | source)
XLA Modules:
  0.0 38.1 jit_solution(12844450063266388230)
XLA Ops:
  0.0 36.2 %shard_map.91 = f32[64,2048]{1,0:T(8,128)} custom-call(bf16[64,2048]{1,0:T(8,128)(2,1)} %rhs.1, bf16[8,256,128]{2,1,0:T(8,128)(2,1)} %basis_hbm.1, s32[8,6]{1,0:T(8,128)} %near_list.1, bf16[8,1536,256]{2,1,0:T(8,128)(2,1)} %bitcast.5, f32[8,128,128]{2,1,0:T(8,128)} %lt_hbm.1, f32[1,14,128,128]{3,2,1,0:T(8,128)} %ct_hbm.1, s32[8,2,15]{2,1,0:T(2,128)} %bitcast.7, ...), custom_call_target="tpu_custom_call" | custom-call | tf_op jit(solution)/shard_map/pallas_call | solution.py:329
  36.2 1.9 %copy.11 = f32[64,2048]{1,0:T(8,128)} copy(f32[64,2048]{1,0:T(8,128)} %shard_map.91) | data formatting | bytes 1048576

commit v2 on v1

--- a/solution.py
+++ b/solution.py
@@ -81,21 +81,28 @@
     lt_load = load(lt_hbm, lt, 12)
     nlist_load = load(near_list, nlist, 13)
     clist_load = load(coupling_list, clist, 14)
+
+    for src in SOURCES:
+        bufs[src][LEAVES] = jnp.zeros((NRHS, RANK), bf16)
+
+    for c in x_loads:
+        c.wait()
+    basis_load.wait()
+    for c in ct_loads:
+        c.wait()
+    lt_load.wait()
     near_loads = [load(near_hbm.at[g], near_w.at[g], 15 + g) for g in range(LEAVES)]
     rc_load = load(rc_hbm, rc, 23)
     coup_loads = [load(coup_hbm.at[g], coup.at[g], 24 + g) for g in range(LEAVES)]
-
-    for src in SOURCES:
-        bufs[src][LEAVES] = jnp.zeros((NRHS, RANK), bf16)
-
-    for c in x_loads:
-        c.wait()
-    basis_load.wait()
     coef = []
     for g in range(LEAVES):
         c = mm(x[LEAVES + g], basis[g])
         coef.append(c)
         own[g] = c.astype(bf16)
+    m0, m1, m2 = [split(ct[i]) for i in range(3)]
+    t = split(mm3(*m0, *m1))
+    t = split(mm3(*t, *m2))
+    t_h[...], t_l[...] = t
 
     def blk_copy(src, dst, i, dy, dz, dc):
         return pltpu.make_async_remote_copy(
@@ -118,16 +125,9 @@
     send("zm", own, (0, 1, 0), whole, 0, -1, 0)
     send("p", own, (0, 0, 1), whole, 0, 0, 1)
 
-    for c in ct_loads:
-        c.wait()
-    lt_load.wait()
     w_h, w_l = split(lt[...].reshape(LEAVES * RANK, RANK))
     lt_h[...] = w_h
     lt_l[...] = w_l
-    m0, m1, m2 = [split(ct[i]) for i in range(3)]
-    t = split(mm3(*m0, *m1))
-    t = split(mm3(*t, *m2))
-    t_h[...], t_l[...] = t
     parts = [split(c) for c in coef]
     c_h = jnp.concatenate([p[0] for p in parts], axis=1)
     c_l = jnp.concatenate([p[1] for p in parts], axis=1)
@@ -174,10 +174,6 @@
     copies["zm"].wait_recv()
     send("zm_fwd", bufs[0, 1, 0], (0, 2, 0), second, 0, -1, 0)
     send("zm_p", bufs[0, 1, 0], (0, 1, 1), whole, 0, 0, 1)
-    copies["y"].wait_recv()
-    send("yzp", bufs[1, 0, 0], (1, -1, 0), whole, 0, 1, 0)
-    send("yzm", bufs[1, 0, 0], (1, 1, 0), whole, 0, -1, 0)
-    send("y_p", bufs[1, 0, 0], (1, 0, 1), whole, 0, 0, 1)
 
     total = share_buf[l]
     for d in range(1, N_LEAF):
@@ -193,6 +189,11 @@
         c.start()
         ag.append(c)
 
+    copies["y"].wait_recv()
+    send("yzp", bufs[1, 0, 0], (1, -1, 0), whole, 0, 1, 0)
+    send("yzm", bufs[1, 0, 0], (1, 1, 0), whole, 0, -1, 0)
+    send("y_p", bufs[1, 0, 0], (1, 0, 1), whole, 0, 0, 1)
+
     clist_load.wait()
     for c in coup_loads:
         c.wait()
@@ -210,20 +211,19 @@
             far_acc[g] = total
             return 0
 
-        lax.fori_loop(0, LEAVES, body, 0)
+        lax.fori_loop(0, LEAVES, body, 0, unroll=2)
 
     copies["p"].wait_recv()
     couple([(0, 0, 1), (1, 0, 0), (0, -1, 0), (0, 1, 0)], True)
 
-    copies["yzp"].wait_recv()
-    send("yzp_fwd", bufs[1, -1, 0], (1, 2, 0), first, 0, 1, 0)
-    send("yzp_p", bufs[1, -1, 0], (1, -1, 1), whole, 0, 0, 1)
-    copies["yzm"].wait_recv()
-    send("yzm_fwd", bufs[1, 1, 0], (1, 2, 0), second, 0, -1, 0)
-    send("yzm_p", bufs[1, 1, 0], (1, 1, 1), whole, 0, 0, 1)
     copies["zp_fwd"].wait_recv()
     copies["zm_fwd"].wait_recv()
+    send("z2_y", bufs[0, 2, 0], (1, 2, 0), whole, 1, 0, 0)
     send("z2_p", bufs[0, 2, 0], (0, 2, 1), whole, 0, 0, 1)
+
+    for name in ("y_p", "zp_p", "zm_p"):
+        copies[name].wait_recv()
+    couple([(1, 0, 1), (0, -1, 1), (0, 1, 1)], False)
 
     rc_load.wait()
     for c in ag:
@@ -240,6 +240,14 @@
         c.start()
         al.append(c)
 
+    g = split(mm3(lt_h[...], lt_l[...], t_h[...], t_l[...]))
+    g_h[...], g_l[...] = g
+
+    copies["yzp"].wait_recv()
+    send("yzp_p", bufs[1, -1, 0], (1, -1, 1), whole, 0, 0, 1)
+    copies["yzm"].wait_recv()
+    send("yzm_p", bufs[1, 1, 0], (1, 1, 1), whole, 0, 0, 1)
+
     nlist_load.wait()
     pl.when(has_down)(up.wait_recv)
     pl.when(has_up)(down.wait_recv)
@@ -250,32 +258,30 @@
         prod[g] = prod[g] + mm(lhs, near_w[g, pl.ds(SIZE, (NEAR - 1) * SIZE), :])
         return 0
 
-    lax.fori_loop(0, LEAVES, near_rest, 0)
-
-    for name in ("y_p", "zp_p", "zm_p"):
+    lax.fori_loop(0, LEAVES, near_rest, 0, unroll=2)
+
+    copies["z2_y"].wait_recv()
+    send("yz2_p", bufs[1, 2, 0], (1, 2, 1), whole, 0, 0, 1)
+
+    for name in ("z2_p", "yzp_p", "yzm_p"):
         copies[name].wait_recv()
-    couple([(1, 0, 1), (0, -1, 1), (0, 1, 1), (1, -1, 0), (1, 1, 0), (0, 2, 0)], False)
-
-    copies["yzp_fwd"].wait_recv()
-    copies["yzm_fwd"].wait_recv()
-    send("yz2_p", bufs[1, 2, 0], (1, 2, 1), whole, 0, 0, 1)
-
-    g = split(mm3(lt_h[...], lt_l[...], t_h[...], t_l[...]))
-    g_h[...], g_l[...] = g
-
-    for name in ("yzp_p", "yzm_p", "z2_p"):
-        copies[name].wait_recv()
-    couple([(1, -1, 1), (1, 1, 1), (0, 2, 1), (1, 2, 0)], False)
-    copies["yz2_p"].wait_recv()
-    couple([(1, 2, 1)], False)
+    couple(
+        [(1, -1, 0), (1, 1, 0), (0, 2, 0), (0, 2, 1), (1, -1, 1), (1, 1, 1), (1, 2, 0)], False
+    )
 
     for c in al:
         c.wait_recv()
     r_h, r_l = split(rf[...].reshape(NRHS, RANK))
     down_leaf = mm3(r_h, r_l, g_h[...], g_l[...], mm_t)
+    for g in range(LEAVES):
+        far_acc[g] = far_acc[g] + down_leaf[:, g * RANK:(g + 1) * RANK]
+    copies["yz2_p"].wait_recv()
+    last = bufs[1, 2, 1]
+    o = (b - blk_of(1, 2, 1) + N_BLK) % N_BLK - 1
     stores = []
     for g in range(LEAVES):
-        leaf_total = (far_acc[g] + down_leaf[:, g * RANK:(g + 1) * RANK]).astype(bf16)
+        lhs = jnp.concatenate([last[clist[g, 0, o]], last[clist[g, 1, o]]], axis=1)
+        leaf_total = (far_acc[g] + mm(lhs, coup[g, o])).astype(bf16)
         prod[g] = prod[g] + mm_t(leaf_total, basis[g])
         c = pltpu.make_async_copy(prod.at[g], out.at[:, pl.ds(g * SIZE, SIZE)], osem.at[g])
         c.start()
@@ -330,7 +336,7 @@
         kernel,
         out_shape=jax.ShapeDtypeStruct((NRHS, LEAVES * SIZE), f32),
         in_specs=[hbm] * 9,
-        out_specs=pl.BlockSpec(memory_space=pltpu.VMEM),
+        out_specs=hbm,
         scratch_shapes=scratch,
         compiler_params=pltpu.CompilerParams(
             collective_id=0, has_side_effects=True, vmem_limit_bytes=67043328

time: 38.2 us -> 32.1 us (0.84)
  Pallas kernels: 36.2 us -> 30.1 us
    pallas_call x1, Pallas kernels: 36.2 us -> 30.1 us  [on_device(): pl.pallas_call(kernel, out_shape=jax.ShapeDtypeStruct((NRHS, LEAVES * SIZ...]
where the time goes in v2:
time: 32.1 us; the launch traced here: 32 us
  Pallas kernels  30.1 us (94%)
  local copies, waits for them, and re-layouts  1.87 us (6%)
    pallas_call x1, Pallas kernels, on_device(): pl.pallas_call(kernel, out_shape=jax.ShapeDtypeStruct((NRHS, LEAVES * SIZ...  30.1 us
    unnamed x1, local copies, waits for them, and re-layouts  1.87 us

profile of v2, /device:TPU:1, one launch (start us, length us, event | category | flops | bytes accessed | tf_op | source)
XLA Modules:
  0.0 32.0 jit_solution(18012557734578526150)
XLA Ops:
  0.0 30.1 %shard_map.91 = f32[64,2048]{1,0:T(8,128)} custom-call(bf16[64,2048]{1,0:T(8,128)(2,1)} %rhs.1, bf16[8,256,128]{2,1,0:T(8,128)(2,1)} %basis_hbm.1, s32[8,6]{1,0:T(8,128)} %near_list.1, bf16[8,1536,256]{2,1,0:T(8,128)(2,1)} %bitcast.5, f32[8,128,128]{2,1,0:T(8,128)} %lt_hbm.1, f32[1,14,128,128]{3,2,1,0:T(8,128)} %ct_hbm.1, s32[8,2,15]{2,1,0:T(2,128)} %bitcast.7, ...), custom_call_target="tpu_custom_call" | custom-call | tf_op jit(solution)/shard_map/pallas_call | solution.py:335
  30.1 1.9 %copy.11 = f32[64,2048]{1,0:T(8,128)} copy(f32[64,2048]{1,0:T(8,128)} %shard_map.91) | data formatting | bytes 1048576

commit v3 on v2

--- a/solution.py
+++ b/solution.py
@@ -41,7 +41,7 @@
     out,
     x, basis, nlist, near_w, lt, ct, clist, coup, rc,
     own, share_buf, rs_buf, root_own, vis, rf, far_acc, prod,
-    lt_h, lt_l, t_h, t_l, g_h, g_l,
+    lt_h, lt_l, t_h, t_l, g_h, g_l, relay_buf, xs, xr,
     *rest,
 ):
     bufs = dict(zip(SOURCES, rest[: len(SOURCES)]))
@@ -63,6 +63,7 @@
         pl.semaphore_signal(barrier, inc=1, device_id={"blk": (b + s) % N_BLK})
     for d in range(1, N_LEAF):
         pl.semaphore_signal(barrier, inc=1, device_id={"leaf": (l + d) % N_LEAF})
+        pl.semaphore_signal(barrier, inc=1, device_id={"blk": blk_of(1, 0, 0), "leaf": (l + d) % N_LEAF})
 
     def load(src, dst, i):
         c = pltpu.make_async_copy(src, dst, lsem.at[i])
@@ -120,7 +121,7 @@
         copies[name] = c
         c.start()
 
-    pl.semaphore_wait(barrier, N_BLK - 1 + N_LEAF - 1)
+    pl.semaphore_wait(barrier, N_BLK - 1 + 2 * (N_LEAF - 1))
     send("zp", own, (0, -1, 0), whole, 0, 1, 0)
     send("zm", own, (0, 1, 0), whole, 0, -1, 0)
     send("p", own, (0, 0, 1), whole, 0, 0, 1)
@@ -155,9 +156,44 @@
         src_ref=x.at[mine], dst_ref=x.at[high], send_sem=hs.at[1], recv_sem=hr.at[1],
         device_id={"leaf": (l + N_LEAF - 1) % N_LEAF},
     )
-    has_up, has_down = l < N_LEAF - 1, l > 0
+    mid = N_LEAF // 2
+    has_up, has_down = (l < N_LEAF - 1) & (l != mid - 1), (l > 0) & (l != mid)
+    crosses = (l == mid - 1) | (l == mid)
+    goes_up = l == mid - 1
+    relays = (l % mid == 0) | (l % mid == mid - 1)
+    relay_up = l % mid == 0
+    y_blk = blk_of(1, 0, 0)
+    relay_leaf = [
+        jnp.where(goes_up, jnp.where(y == h, mid, 0), jnp.where(y == h, mid - 1, N_LEAF - 1)) for h in range(2)
+    ]
+    crossing = [
+        pltpu.make_async_remote_copy(
+            src_ref=x.at[pl.ds(LEAVES + h * (LEAVES // 2), LEAVES // 2)], dst_ref=relay_buf,
+            send_sem=xs.at[h], recv_sem=xr.at[0], device_id={"blk": y_blk, "leaf": relay_leaf[h]},
+        )
+        for h in range(2)
+    ]
+    half = jnp.where(relay_up, (y == 1) == (l == 0), (y == 1) != (l == mid - 1)).astype(jnp.int32)
+    relay_to = jnp.where(relay_up, 0, 2 * LEAVES) + half * (LEAVES // 2)
+    relayed = pltpu.make_async_remote_copy(
+        src_ref=relay_buf, dst_ref=x.at[pl.ds(relay_to, LEAVES // 2)],
+        send_sem=xs.at[2], recv_sem=xr.at[1 + half],
+        device_id={"blk": y_blk, "leaf": jnp.where(relay_up, mid, mid - 1)},
+    )
+    arrivals = [
+        pltpu.make_async_remote_copy(
+            src_ref=relay_buf, dst_ref=x.at[pl.ds(jnp.where(goes_up, 2 * LEAVES, 0) + h * (LEAVES // 2), LEAVES // 2)],
+            send_sem=xs.at[2], recv_sem=xr.at[1 + h], device_id={"blk": y_blk, "leaf": l},
+        )
+        for h in range(2)
+    ]
     pl.when(has_up)(up.start)
     pl.when(has_down)(down.start)
+
+    @pl.when(crosses)
+    def _():
+        for c in crossing:
+            c.start()
 
     for c in near_loads:
         c.wait()
@@ -240,6 +276,11 @@
         c.start()
         al.append(c)
 
+    @pl.when(relays)
+    def _():
+        crossing[0].wait_recv()
+        relayed.start()
+
     g = split(mm3(lt_h[...], lt_l[...], t_h[...], t_l[...]))
     g_h[...], g_l[...] = g
 
@@ -251,6 +292,12 @@
     nlist_load.wait()
     pl.when(has_down)(up.wait_recv)
     pl.when(has_up)(down.wait_recv)
+
+    @pl.when(crosses)
+    def _():
+        for c in arrivals:
+            c.wait_recv()
+
     base = (b * N_LEAF + l) * LEAVES - LEAVES
 
     def near_rest(g, _):
@@ -291,6 +338,13 @@
         c.wait_send()
     pl.when(has_up)(up.wait_send)
     pl.when(has_down)(down.wait_send)
+
+    @pl.when(crosses)
+    def _():
+        for c in crossing:
+            c.wait_send()
+
+    pl.when(relays)(relayed.wait_send)
     for c in stores:
         c.wait()
 
@@ -326,6 +380,7 @@
         V((LEAVES * RANK, RANK), bf16),
         V((LEAVES * RANK, RANK), bf16),
     ]
+    scratch += [V((LEAVES // 2, NRHS, SIZE), bf16), dma((3,)), dma((3,))]
     scratch += [V((LEAVES + 1, NRHS, RANK), bf16) for _ in SOURCES]
     scratch += [
         dma((32,)), dma((LEAVES,)), S.REGULAR, dma((2,)), dma((2,)), dma((17,)), dma((17,)),

time: 32.1 us -> 29.8 us (0.928); the launches traced: 32 us -> 29.2 us
  Pallas kernels: 30.1 us -> 27.3 us
    pallas_call x1, Pallas kernels: 30.1 us -> 27.3 us  [on_device(): pl.pallas_call(kernel, out_shape=jax.ShapeDtypeStruct((NRHS, LEAVES * SIZ...]
where the time goes in v3:
time: 29.8 us; the launch traced here: 29.2 us
  Pallas kernels  27.3 us (92%)
  local copies, waits for them, and re-layouts  1.87 us (6%)
    pallas_call x1, Pallas kernels, on_device(): pl.pallas_call(kernel, out_shape=jax.ShapeDtypeStruct((NRHS, LEAVES * SIZ...  27.3 us
    unnamed x1, local copies, waits for them, and re-layouts  1.87 us

profile of v3, /device:TPU:1, one launch (start us, length us, event | category | flops | bytes accessed | tf_op | source)
XLA Modules:
  0.0 29.2 jit_solution(11535102106983083548)
XLA Ops:
  0.0 27.3 %shard_map.91 = f32[64,2048]{1,0:T(8,128)} custom-call(bf16[64,2048]{1,0:T(8,128)(2,1)} %rhs.1, bf16[8,256,128]{2,1,0:T(8,128)(2,1)} %basis_hbm.1, s32[8,6]{1,0:T(8,128)} %near_list.1, bf16[8,1536,256]{2,1,0:T(8,128)(2,1)} %bitcast.5, f32[8,128,128]{2,1,0:T(8,128)} %lt_hbm.1, f32[1,14,128,128]{3,2,1,0:T(8,128)} %ct_hbm.1, s32[8,2,15]{2,1,0:T(2,128)} %bitcast.7, ...), custom_call_target="tpu_custom_call" | custom-call | tf_op jit(solution)/shard_map/pallas_call | solution.py:390
  27.3 1.9 %copy.11 = f32[64,2048]{1,0:T(8,128)} copy(f32[64,2048]{1,0:T(8,128)} %shard_map.91) | data formatting | bytes 1048576

commit v4 on v3

--- a/solution.py
+++ b/solution.py
@@ -168,24 +168,35 @@
     ]
     crossing = [
         pltpu.make_async_remote_copy(
-            src_ref=x.at[pl.ds(LEAVES + h * (LEAVES // 2), LEAVES // 2)], dst_ref=relay_buf,
-            send_sem=xs.at[h], recv_sem=xr.at[0], device_id={"blk": y_blk, "leaf": relay_leaf[h]},
-        )
-        for h in range(2)
+            src_ref=x.at[pl.ds(LEAVES + h * (LEAVES // 2) + 2 * q, 2)], dst_ref=relay_buf.at[pl.ds(2 * q, 2)],
+            send_sem=xs.at[2 * q + h], recv_sem=xr.at[q], device_id={"blk": y_blk, "leaf": relay_leaf[h]},
+        )
+        for q in range(2) for h in range(2)
     ]
     half = jnp.where(relay_up, (y == 1) == (l == 0), (y == 1) != (l == mid - 1)).astype(jnp.int32)
     relay_to = jnp.where(relay_up, 0, 2 * LEAVES) + half * (LEAVES // 2)
-    relayed = pltpu.make_async_remote_copy(
-        src_ref=relay_buf, dst_ref=x.at[pl.ds(relay_to, LEAVES // 2)],
-        send_sem=xs.at[2], recv_sem=xr.at[1 + half],
-        device_id={"blk": y_blk, "leaf": jnp.where(relay_up, mid, mid - 1)},
-    )
+    relayed = [
+        pltpu.make_async_remote_copy(
+            src_ref=relay_buf.at[pl.ds(2 * q, 2)], dst_ref=x.at[pl.ds(relay_to + 2 * q, 2)],
+            send_sem=xs.at[4 + q], recv_sem=xr.at[2 + 2 * q + half],
+            device_id={"blk": y_blk, "leaf": jnp.where(relay_up, mid, mid - 1)},
+        )
+        for q in range(2)
+    ]
+
+    def relay(q):
+        @pl.when(relays)
+        def _():
+            crossing[2 * q].wait_recv()
+            relayed[q].start()
+
     arrivals = [
         pltpu.make_async_remote_copy(
-            src_ref=relay_buf, dst_ref=x.at[pl.ds(jnp.where(goes_up, 2 * LEAVES, 0) + h * (LEAVES // 2), LEAVES // 2)],
-            send_sem=xs.at[2], recv_sem=xr.at[1 + h], device_id={"blk": y_blk, "leaf": l},
-        )
-        for h in range(2)
+            src_ref=relay_buf.at[pl.ds(2 * q, 2)],
+            dst_ref=x.at[pl.ds(jnp.where(goes_up, 2 * LEAVES, 0) + h * (LEAVES // 2) + 2 * q, 2)],
+            send_sem=xs.at[4 + q], recv_sem=xr.at[2 + 2 * q + h], device_id={"blk": y_blk, "leaf": l},
+        )
+        for q in range(2) for h in range(2)
     ]
     pl.when(has_up)(up.start)
     pl.when(has_down)(down.start)
@@ -257,6 +268,7 @@
     send("z2_y", bufs[0, 2, 0], (1, 2, 0), whole, 1, 0, 0)
     send("z2_p", bufs[0, 2, 0], (0, 2, 1), whole, 0, 0, 1)
 
+    relay(0)
     for name in ("y_p", "zp_p", "zm_p"):
         copies[name].wait_recv()
     couple([(1, 0, 1), (0, -1, 1), (0, 1, 1)], False)
@@ -276,10 +288,7 @@
         c.start()
         al.append(c)
 
-    @pl.when(relays)
-    def _():
-        crossing[0].wait_recv()
-        relayed.start()
+    relay(1)
 
     g = split(mm3(lt_h[...], lt_l[...], t_h[...], t_l[...]))
     g_h[...], g_l[...] = g
@@ -344,7 +353,11 @@
         for c in crossing:
             c.wait_send()
 
-    pl.when(relays)(relayed.wait_send)
+    @pl.when(relays)
+    def _():
+        for c in relayed:
+            c.wait_send()
+
     for c in stores:
         c.wait()
 
@@ -380,7 +393,7 @@
         V((LEAVES * RANK, RANK), bf16),
         V((LEAVES * RANK, RANK), bf16),
     ]
-    scratch += [V((LEAVES // 2, NRHS, SIZE), bf16), dma((3,)), dma((3,))]
+    scratch += [V((LEAVES // 2, NRHS, SIZE), bf16), dma((6,)), dma((6,))]
     scratch += [V((LEAVES + 1, NRHS, RANK), bf16) for _ in SOURCES]
     scratch += [
         dma((32,)), dma((LEAVES,)), S.REGULAR, dma((2,)), dma((2,)), dma((17,)), dma((17,)),

time: 29.8 us -> 29.4 us (0.987); the launches traced: 29.2 us -> 29.3 us
  no operation moved by 1% of the time
where the time goes in v4:
time: 29.4 us; the launch traced here: 29.3 us
  Pallas kernels  27.4 us (93%)
  local copies, waits for them, and re-layouts  1.87 us (6%)
    pallas_call x1, Pallas kernels, on_device(): pl.pallas_call(kernel, out_shape=jax.ShapeDtypeStruct((NRHS, LEAVES * SIZ...  27.4 us
    unnamed x1, local copies, waits for them, and re-layouts  1.87 us

profile of v4, /device:TPU:1, one launch (start us, length us, event | category | flops | bytes accessed | tf_op | source)
XLA Modules:
  0.0 29.3 jit_solution(17105966658479152450)
XLA Ops:
  0.0 27.4 %shard_map.91 = f32[64,2048]{1,0:T(8,128)} custom-call(bf16[64,2048]{1,0:T(8,128)(2,1)} %rhs.1, bf16[8,256,128]{2,1,0:T(8,128)(2,1)} %basis_hbm.1, s32[8,6]{1,0:T(8,128)} %near_list.1, bf16[8,1536,256]{2,1,0:T(8,128)(2,1)} %bitcast.5, f32[8,128,128]{2,1,0:T(8,128)} %lt_hbm.1, f32[1,14,128,128]{3,2,1,0:T(8,128)} %ct_hbm.1, s32[8,2,15]{2,1,0:T(2,128)} %bitcast.7, ...), custom_call_target="tpu_custom_call" | custom-call | tf_op jit(solution)/shard_map/pallas_call | solution.py:403
  27.4 1.9 %copy.11 = f32[64,2048]{1,0:T(8,128)} copy(f32[64,2048]{1,0:T(8,128)} %shard_map.91) | data formatting | bytes 1048576
